TPU v7x, 32 devices: a whole 2x2x4 slice. The times are simulated.
32 devices in a mesh: dp: 2 (over core), head: 4 (over y, x), seq: 4 (over z).
Axes of the slice: x: 2, y: 2, z: 4, core: 2. Of those that a mesh axis runs over, the one named last changes fastest.
Arguments:
- layer_input: bfloat16 [2, 2048, 2048], P('dp', 'seq'), may hold values from -6 to 6
- head_values: bfloat16 [2, 2048, 2048], P('dp', 'seq', 'head'), may hold values from -6 to 6
- dt_raw: float32 [2, 32, 2048], P('dp', 'head', 'seq'), may hold values from -2 to 40
- w_bc: bfloat16 [2048, 128], replicated, may hold values from -0.015625 to 0.015625
- decay_rate: float32 [32], P('head'), may hold values from 0.0068359375 to 2
- dt_bias: float32 [32], P('head'), may hold values from -4.5 to -3.5
- skip_gain: float32 [32], P('head'), may hold values from 0.5 to 1.5
- grad_y: bfloat16 [2, 2048, 2048], P('dp', 'seq', 'head'), may hold values from -6 to 6
Outputs:
- y_out: bfloat16 [2, 2048, 2048], P('dp', 'seq', 'head')
- grad_values: bfloat16 [2, 2048, 2048], P('dp', 'seq', 'head')
- grad_input: bfloat16 [2, 2048, 2048], P('dp', 'seq')
- grad_w_bc: float32 [2048, 128], P(('dp', 'seq'))
All inputs are finite; a program needn't handle non-finite values.
Results may differ from a plain program's by a relative error of at most 0.013.
Values may be sent and summed in bfloat16 or wider, within the bound.
No kernel may reach another device: no remote copies, remote signals or barrier semaphores. Data moves between devices by JAX's collectives and lax.ppermute only.
A program may use at most 320 MiB of HBM per device.

v0:
```python
import jax
import jax.numpy as jnp
from jax import lax
from jax.sharding import PartitionSpec as P

maximum_level = lax.Precision.HIGHEST


def carried_in(x, axis, combine, identity, reverse):
    size, here = (lax.axis_size(axis), lax.axis_index(axis))
    everything = jax.tree.map(
        lambda part, kind: lax.all_gather(part.astype(kind), axis), x, (jnp.bfloat16, jnp.bfloat16)
    )
    start = jax.tree.map(
        lambda part, zero: jnp.broadcast_to(jnp.asarray(zero, part.dtype), part.shape), x, identity
    )

    def step(k, before):
        at = size - 1 - k if reverse else k
        reached = at > here if reverse else at < here
        new = combine(
            before, jax.tree.map(lambda part, own: part[at].astype(own.dtype), everything, x)
        )
        return jax.tree.map(lambda a, b: jnp.where(reached, a, b), new, before)

    return lax.fori_loop(0, size, step, start)


def spread_heads(vector):
    return vector[None, :, None, None]


def combine_states(earlier, later_part):
    factor_vec = later_part[0]
    return (earlier[0] * factor_vec, spread_heads(factor_vec) * earlier[1] + later_part[1])


def head_state(scaled_keys, value_matrix):
    return jnp.einsum("qgz,qgn->gzn", scaled_keys, value_matrix, precision=maximum_level)


def spread_state(value_scaled, key_rows):
    return jnp.einsum("shp,sn->hnp", value_scaled, key_rows, precision=maximum_level)


def shared_query(query_rows, state):
    return jnp.einsum("tn,hnp->thp", query_rows, state, precision=maximum_level)


def head_query(query_rows, state):
    return jnp.einsum("thp,hnp->tn", query_rows, state, precision=maximum_level)


def per_device(layer_input, head_values, dt_raw, w_bc, decay_rate, dt_bias, skip_gain, grad_y):
    tokens = layer_input[0]
    head_count = decay_rate.shape[0]
    length = tokens.shape[0]
    state_dim = w_bc.shape[1] // 2
    head_dim = head_values.shape[2] // head_count
    values_x = head_values[0].reshape(length, head_count, head_dim)
    cotangent = grad_y[0].reshape(length, head_count, head_dim)
    log_step = -decay_rate[:, None] * jax.nn.softplus(dt_raw[0] + dt_bias[:, None])
    cum_log = jnp.cumsum(log_step, axis=1)
    prev_log = cum_log - log_step
    final_logarithm = cum_log[:, -1]
    projected = jnp.dot(tokens, w_bc, preferred_element_type=jnp.float32).astype(jnp.bfloat16)
    b_mat = projected[:, :state_dim]
    c_mat = projected[:, state_dim:]
    row_index = jnp.arange(length)[:, None]
    col_index = jnp.arange(length)[None, :]
    state_scores = jnp.einsum("tn,sn->ts", c_mat, b_mat, preferred_element_type=jnp.float32)

    def head_block(totals, inputs):
        cum_head, prev_head, x_head, g_head = inputs
        diff_fwd = cum_head[:, None] - cum_head[None, :]
        diff_bwd = prev_head[None, :] - prev_head[:, None]
        exponent = jnp.minimum(jnp.where(col_index < row_index, diff_fwd, diff_bwd), 0.0)
        kernel = jnp.where(col_index == row_index, 0.0, jnp.exp(exponent))
        weights_main = (state_scores * kernel).astype(jnp.bfloat16)
        value_scores = jnp.dot(g_head, x_head.T, preferred_element_type=jnp.float32)
        weights_grad = (value_scores * kernel).astype(jnp.bfloat16)
        y_head = jnp.dot(weights_main, x_head, preferred_element_type=jnp.float32)
        gv_head = jnp.dot(weights_main.T, g_head, preferred_element_type=jnp.float32)
        gc_total = totals[0] + jnp.dot(weights_grad, b_mat, preferred_element_type=jnp.float32)
        gb_total = totals[1] + jnp.dot(weights_grad.T, c_mat, preferred_element_type=jnp.float32)
        return ((gc_total, gb_total), (y_head, gv_head))

    zero_rows = jnp.zeros((length, state_dim), jnp.float32)
    head_inputs = (cum_log, prev_log, values_x.transpose(1, 0, 2), cotangent.transpose(1, 0, 2))
    (local_gc, local_gb), (heads_y, heads_gv) = lax.scan(
        head_block, (zero_rows, zero_rows), head_inputs
    )
    local_y = heads_y.transpose(1, 0, 2)
    local_gv = heads_gv.transpose(1, 0, 2)
    b_float = b_mat.astype(jnp.float32)
    c_float = c_mat.astype(jnp.float32)
    x_float = values_x.astype(jnp.float32)
    g_float = cotangent.astype(jnp.float32)
    up_cum = jnp.exp(cum_log).T
    up_prev = jnp.exp(prev_log).T
    down_cum = jnp.exp(final_logarithm[:, None] - cum_log).T
    down_prev = jnp.exp(final_logarithm[:, None] - prev_log).T
    next_main = head_state(b_float[:, None, :] * down_cum[:, :, None], x_float)
    prior_main = head_state(b_float[:, None, :] * up_prev[:, :, None], x_float)
    next_back = head_state(c_float[:, None, :] * down_prev[:, :, None], g_float)
    prior_back = head_state(c_float[:, None, :] * up_cum[:, :, None], g_float)
    next_gc = spread_state(x_float * down_cum[:, :, None], b_float)
    prior_gc = spread_state(x_float * up_prev[:, :, None], b_float)
    next_gb = spread_state(g_float * down_prev[:, :, None], c_float)
    prior_gb = spread_state(g_float * up_cum[:, :, None], c_float)
    stacked_next = jnp.stack([next_main, next_back, next_gc, next_gb])
    stacked_prior = jnp.stack([prior_main, prior_back, prior_gc, prior_gb])
    state_pick = (0, 1, 2, 3)
    decay_total = jnp.exp(final_logarithm)
    unit_decay = jnp.ones_like(decay_total)
    zero_stack = jnp.zeros_like(stacked_next)
    scanned_next = carried_in(
        (decay_total, stacked_next), "seq", combine_states, (unit_decay, zero_stack), False
    )
    scanned_prior = carried_in(
        (decay_total, stacked_prior), "seq", combine_states, (unit_decay, zero_stack), True
    )
    contribution_earlier = scanned_next[1]
    contribution_later = scanned_prior[1]
    before_list = [contribution_earlier[slot_index] for slot_index in state_pick]
    after_list = [contribution_later[slot_index] for slot_index in state_pick]
    carry_y = (
        shared_query(c_float, before_list[0]) * up_cum[:, :, None]
        + shared_query(c_float, after_list[0]) * down_prev[:, :, None]
    )
    carry_gv = (
        shared_query(b_float, before_list[1]) * up_prev[:, :, None]
        + shared_query(b_float, after_list[1]) * down_cum[:, :, None]
    )
    carry_gc = head_query(g_float * up_cum[:, :, None], before_list[2]) + head_query(
        g_float * down_prev[:, :, None], after_list[2]
    )
    carry_gb = head_query(x_float * up_prev[:, :, None], before_list[3]) + head_query(
        x_float * down_cum[:, :, None], after_list[3]
    )
    y_out = (local_y + carry_y + skip_gain[None, :, None] * x_float).astype(jnp.bfloat16)
    grad_values = (local_gv + carry_gv + skip_gain[None, :, None] * g_float).astype(jnp.bfloat16)
    partial_bc = jnp.concatenate([local_gb + carry_gb, local_gc + carry_gc], axis=1)
    summed_bc = lax.psum(partial_bc.astype(jnp.bfloat16), "head")
    grad_input = jnp.einsum(
        "tk,dk->td", summed_bc, w_bc, preferred_element_type=jnp.float32
    ).astype(jnp.bfloat16)
    group_count = lax.axis_size("dp") * lax.axis_size("seq")
    total_tokens = group_count * length
    weight_part = lax.psum_scatter(
        jnp.einsum("td,tk->dk", tokens, summed_bc, preferred_element_type=jnp.float32),
        ("dp", "seq"),
        scatter_dimension=0,
        tiled=True,
    )
    grad_w_bc = weight_part / total_tokens
    return (
        y_out.reshape(1, length, head_count * head_dim),
        grad_values.reshape(1, length, head_count * head_dim),
        grad_input[None],
        grad_w_bc,
    )


def solution(mesh):
    in_specs = (
        P("dp", "seq", None),
        P("dp", "seq", "head"),
        P("dp", "head", "seq"),
        P(),
        P("head"),
        P("head"),
        P("head"),
        P("dp", "seq", "head"),
    )
    out_specs = (
        P("dp", "seq", "head"),
        P("dp", "seq", "head"),
        P("dp", "seq", None),
        P(("dp", "seq"), None),
    )
    return jax.shard_map(
        per_device, mesh=mesh, in_specs=in_specs, out_specs=out_specs, check_vma=False
    )
```

profile of v0, /device:TPU:0, one launch (start us, length us, event | category | flops | bytes accessed | tf_op | source)
XLA Modules:
  0.0 231.7 jit_solution(15547888984841466233)
XLA Ops:
  16.3 2.2 fusion.33
  30.8 56.7 %while.50 = (s32[]{:T(128)}, f32[512,64]{0,1:T(8,128)S(1)}, f32[512,64]{0,1:T(8,128)S(1)}, f32[8,512,64]{1,2,0:T(8,128)}, f32[8,512,64]{1,2,0:T(8,128)}, /*index...) while((s32[]{:T(128)}, f32[512,64]{0,1:T(8,128)S(1)}, ...), condition=%wide.region_3.4_spmd.clone.clone, body=%wide.region_2.3_spmd.clone.clone.sunk | while | flops 174981120 | bytes 13274344 | solution.py:90
  33.5 2.4 %fusion.139 = f32[8,512,64]{1,2,0:T(8,128)} fusion(f32[8,512,64]{1,2,0:T(8,128)} %get-tuple-element.700, s32[]{:T(128)} %get-tuple-element.697, bf16[8,512,64]{1,2,0:T(8,128)(2,1)} %copy-done.1, f32[512,512]{1,0:T(8,128)} %get-tuple-element.722, f32[512]{0:T(512)S(1)} %bitcast.267, f32[512]{0:T(512)S(1)} %bitcast.270), kind=kOutput, calls=%fused_computation.15.clone.1 | convolution fusion | flops 35913728 | bytes 1254400 | tf_op jit(solution)/shard_map/while/body/eval_jaxpr/dot_general | solution.py:82
  40.6 2.4 %fusion.139 = f32[8,512,64]{1,2,0:T(8,128)} fusion(f32[8,512,64]{1,2,0:T(8,128)} %get-tuple-element.700, s32[]{:T(128)} %get-tuple-element.697, bf16[8,512,64]{1,2,0:T(8,128)(2,1)} %copy-done.1, f32[512,512]{1,0:T(8,128)} %get-tuple-element.722, f32[512]{0:T(512)S(1)} %bitcast.267, f32[512]{0:T(512)S(1)} %bitcast.270), kind=kOutput, calls=%fused_computation.15.clone.1 | convolution fusion | flops 35913728 | bytes 1254400 | tf_op jit(solution)/shard_map/while/body/eval_jaxpr/dot_general | solution.py:82
  43.0 2.0 fusion.140
  47.7 2.4 %fusion.139 = f32[8,512,64]{1,2,0:T(8,128)} fusion(f32[8,512,64]{1,2,0:T(8,128)} %get-tuple-element.700, s32[]{:T(128)} %get-tuple-element.697, bf16[8,512,64]{1,2,0:T(8,128)(2,1)} %copy-done.1, f32[512,512]{1,0:T(8,128)} %get-tuple-element.722, f32[512]{0:T(512)S(1)} %bitcast.267, f32[512]{0:T(512)S(1)} %bitcast.270), kind=kOutput, calls=%fused_computation.15.clone.1 | convolution fusion | flops 35913728 | bytes 1254400 | tf_op jit(solution)/shard_map/while/body/eval_jaxpr/dot_general | solution.py:82
  50.1 2.0 fusion.140
  54.8 2.4 %fusion.139 = f32[8,512,64]{1,2,0:T(8,128)} fusion(f32[8,512,64]{1,2,0:T(8,128)} %get-tuple-element.700, s32[]{:T(128)} %get-tuple-element.697, bf16[8,512,64]{1,2,0:T(8,128)(2,1)} %copy-done.1, f32[512,512]{1,0:T(8,128)} %get-tuple-element.722, f32[512]{0:T(512)S(1)} %bitcast.267, f32[512]{0:T(512)S(1)} %bitcast.270), kind=kOutput, calls=%fused_computation.15.clone.1 | convolution fusion | flops 35913728 | bytes 1254400 | tf_op jit(solution)/shard_map/while/body/eval_jaxpr/dot_general | solution.py:82
  57.2 2.0 fusion.140
  61.9 2.4 %fusion.139 = f32[8,512,64]{1,2,0:T(8,128)} fusion(f32[8,512,64]{1,2,0:T(8,128)} %get-tuple-element.700, s32[]{:T(128)} %get-tuple-element.697, bf16[8,512,64]{1,2,0:T(8,128)(2,1)} %copy-done.1, f32[512,512]{1,0:T(8,128)} %get-tuple-element.722, f32[512]{0:T(512)S(1)} %bitcast.267, f32[512]{0:T(512)S(1)} %bitcast.270), kind=kOutput, calls=%fused_computation.15.clone.1 | convolution fusion | flops 35913728 | bytes 1254400 | tf_op jit(solution)/shard_map/while/body/eval_jaxpr/dot_general | solution.py:82
  64.3 2.0 fusion.140
  69.0 2.4 %fusion.139 = f32[8,512,64]{1,2,0:T(8,128)} fusion(f32[8,512,64]{1,2,0:T(8,128)} %get-tuple-element.700, s32[]{:T(128)} %get-tuple-element.697, bf16[8,512,64]{1,2,0:T(8,128)(2,1)} %copy-done.1, f32[512,512]{1,0:T(8,128)} %get-tuple-element.722, f32[512]{0:T(512)S(1)} %bitcast.267, f32[512]{0:T(512)S(1)} %bitcast.270), kind=kOutput, calls=%fused_computation.15.clone.1 | convolution fusion | flops 35913728 | bytes 1254400 | tf_op jit(solution)/shard_map/while/body/eval_jaxpr/dot_general | solution.py:82
  71.3 2.0 fusion.140
  76.0 2.4 %fusion.139 = f32[8,512,64]{1,2,0:T(8,128)} fusion(f32[8,512,64]{1,2,0:T(8,128)} %get-tuple-element.700, s32[]{:T(128)} %get-tuple-element.697, bf16[8,512,64]{1,2,0:T(8,128)(2,1)} %copy-done.1, f32[512,512]{1,0:T(8,128)} %get-tuple-element.722, f32[512]{0:T(512)S(1)} %bitcast.267, f32[512]{0:T(512)S(1)} %bitcast.270), kind=kOutput, calls=%fused_computation.15.clone.1 | convolution fusion | flops 35913728 | bytes 1254400 | tf_op jit(solution)/shard_map/while/body/eval_jaxpr/dot_general | solution.py:82
  78.4 2.0 fusion.140
  83.1 2.4 %fusion.139 = f32[8,512,64]{1,2,0:T(8,128)} fusion(f32[8,512,64]{1,2,0:T(8,128)} %get-tuple-element.700, s32[]{:T(128)} %get-tuple-element.697, bf16[8,512,64]{1,2,0:T(8,128)(2,1)} %copy-done.1, f32[512,512]{1,0:T(8,128)} %get-tuple-element.722, f32[512]{0:T(512)S(1)} %bitcast.267, f32[512]{0:T(512)S(1)} %bitcast.270), kind=kOutput, calls=%fused_computation.15.clone.1 | convolution fusion | flops 35913728 | bytes 1254400 | tf_op jit(solution)/shard_map/while/body/eval_jaxpr/dot_general | solution.py:82
  85.5 2.0 fusion.140
  90.0 2.7 %convert_multiply_fusion.7 = (f32[1,512,512]{1,2,0:T(8,128)}, f32[1,512,512]{1,2,0:T(8,128)}) fusion(bf16[1,512,512]{1,2,0:T(8,128)(2,1)} %bitcast.250, f32[512,8]{0,1:T(8,128)S(1)} %copy-done.15, f32[512,8]{0,1:T(8,128)} %copy-done.19), kind=kLoop, calls=%fused_computation.46 | loop fusion | flops 786432 | bytes 2654208 | tf_op jit(solution)/shard_map/mul | solution.py:110
  96.4 14.6 %all-reduce = bf16[32]{0:T(256)(128)(2,1)} all-reduce(bf16[32]{0:T(256)(128)(2,1)} %dynamic-update-slice), channel_id=2, replica_groups=mesh['dp'=2,'head'=4,'seq'=4] {'seq'}, use_global_device_ids=true, to_apply=%add | all-reduce | flops 32 | bytes 128
  112.4 15.4 %while.49 = (s32[]{:T(128)}, f32[4,8,64,64]{3,2,1,0:T(8,128)}, s32[]{:T(128)}, bf16[4,8]{1,0:T(4,128)(2,1)}, bf16[4,4,8,64,64]{4,3,2,1,0:T(8,128)(2,1)}, /*index=5*/s32[]{:T(128)}, s32[]{:T(128)}, s32[]{:T(128)}, s32[]{:T(128)}) while((s32[]{:T(128)}, f32[4,8,64,64]{3,2,1,0:T(8,128)}, s32[]{:T(128)}, bf16[4,8]{1,0:T(4,128)(2,1)}, ...), condition=%wide.region_7.8_spmd.clone, body=%wide.region_6.7_spmd.clone.sunk | while | flops 655376 | bytes 1310967 | solution.py:26
  113.6 2.4 %fusion.129 = f32[4,8,64,64]{3,2,1,0:T(8,128)} fusion(f32[4,8,64,64]{3,2,1,0:T(8,128)} %get-tuple-element.735, bf16[4,4,8,64,64]{4,3,2,1,0:T(8,128)(2,1)} %get-tuple-element.747, s32[]{:T(128)S(6)} %select_n.121, f32[8]{0:T(128)} %bitcast_convert_fusion.5, pred[]{:T(512)S(6)} %compare.10, pred[]{:T(512)S(6)} %gt.12), kind=kLoop, calls=%fused_computation.6.clone.1 | loop fusion | flops 655360 | bytes 1310758 | tf_op jit(solution)/shard_map/while/body/eval_jaxpr/jit(_where)/select_n | solution.py:24
  117.1 2.7 %fusion.129 = f32[4,8,64,64]{3,2,1,0:T(8,128)} fusion(f32[4,8,64,64]{3,2,1,0:T(8,128)} %get-tuple-element.735, bf16[4,4,8,64,64]{4,3,2,1,0:T(8,128)(2,1)} %get-tuple-element.747, s32[]{:T(128)S(6)} %select_n.121, f32[8]{0:T(128)} %bitcast_convert_fusion.5, pred[]{:T(512)S(6)} %compare.10, pred[]{:T(512)S(6)} %gt.12), kind=kLoop, calls=%fused_computation.6.clone.1 | loop fusion | flops 655360 | bytes 1310758 | tf_op jit(solution)/shard_map/while/body/eval_jaxpr/jit(_where)/select_n | solution.py:24
  121.1 2.7 %fusion.129 = f32[4,8,64,64]{3,2,1,0:T(8,128)} fusion(f32[4,8,64,64]{3,2,1,0:T(8,128)} %get-tuple-element.735, bf16[4,4,8,64,64]{4,3,2,1,0:T(8,128)(2,1)} %get-tuple-element.747, s32[]{:T(128)S(6)} %select_n.121, f32[8]{0:T(128)} %bitcast_convert_fusion.5, pred[]{:T(512)S(6)} %compare.10, pred[]{:T(512)S(6)} %gt.12), kind=kLoop, calls=%fused_computation.6.clone.1 | loop fusion | flops 655360 | bytes 1310758 | tf_op jit(solution)/shard_map/while/body/eval_jaxpr/jit(_where)/select_n | solution.py:24
  125.0 2.7 %fusion.129 = f32[4,8,64,64]{3,2,1,0:T(8,128)} fusion(f32[4,8,64,64]{3,2,1,0:T(8,128)} %get-tuple-element.735, bf16[4,4,8,64,64]{4,3,2,1,0:T(8,128)(2,1)} %get-tuple-element.747, s32[]{:T(128)S(6)} %select_n.121, f32[8]{0:T(128)} %bitcast_convert_fusion.5, pred[]{:T(512)S(6)} %compare.10, pred[]{:T(512)S(6)} %gt.12), kind=kLoop, calls=%fused_computation.6.clone.1 | loop fusion | flops 655360 | bytes 1310758 | tf_op jit(solution)/shard_map/while/body/eval_jaxpr/jit(_where)/select_n | solution.py:24
  127.7 10.7 %while.48 = (s32[]{:T(128)}, f32[4,8,64,64]{3,2,1,0:T(8,128)S(1)}, s32[]{:T(128)}, bf16[4,8]{1,0:T(4,128)(2,1)}, bf16[4,4,8,64,64]{4,3,2,1,0:T(8,128)(2,1)}, /*index=5*/s32[]{:T(128)}, s32[]{:T(128)}) while((s32[]{:T(128)}, f32[4,8,64,64]{3,2,1,0:T(8,128)S(1)}, s32[]{:T(128)}, bf16[4,8]{1,0:T(4,128)(2,1)}, ...), condition=%wide.region_5.6_spmd.clone, body=%wide.region_4.5_spmd.clone.sunk | while | flops 655372 | bytes 1310905 | solution.py:26
  138.4 2.2 convolution_bitcast_fusion.5
  140.6 2.1 convolution_bitcast_fusion.3
  148.0 37.3 %all-reduce.3.cloned.1.call-done = bf16[512,128]{0,1:T(8,128)(2,1)} async-done(((bf16[512,128]{0,1:T(8,128)(2,1)}), bf16[512,128]{0,1:T(8,128)(2,1)}) %all-reduce.3.cloned.1.call-update) | async-done | bytes 131088 | tf_op jit(solution)/shard_map/psum | solution.py:144
  185.3 2.4 %convolution_bitcast_fusion.2 = f32[2048,128]{0,1:T(8,128)} fusion(bf16[512,128]{0,1:T(8,128)(2,1)} %all-reduce.3.cloned.1.call-done, bf16[1,512,2048]{2,1,0:T(8,128)(2,1)S(1)} %copy-done), kind=kOutput, calls=%fused_computation.35 | convolution fusion | flops 268435456 | bytes 3276800 | tf_op jit(solution)/shard_map/td,tk->dk/dot_general | solution.py:151
  191.2 2.3 fusion.44
  195.6 3.1 %fusion.20 = bf16[1,512,2048]{2,1,0:T(8,128)(2,1)} fusion(bf16[512,128]{0,1:T(8,128)(2,1)S(1)} %copy-done.12, bf16[2048,128]{1,0:T(8,128)(2,1)} %param.17), kind=kOutput, calls=%fused_computation.34 | convolution fusion | flops 269484032 | bytes 2752512 | tf_op jit(solution)/shard_map/tk,dk->td/dot_general | solution.py:145
  198.6 24.9 %reduce-scatter.2.cloned.1.call-done = f32[256,128]{0,1:T(8,128)} async-done(((f32[2048,128]{0,1:T(8,128)}), f32[256,128]{0,1:T(8,128)}) %reduce-scatter.2.cloned.1.call-update) | async-done | bytes 131088 | tf_op jit(solution)/shard_map/reduce_scatter | solution.py:150
  (202 shorter events, 79.0 us)
Async XLA Ops:
  7.2 4.8 %copy-start = (bf16[1,512,2048]{2,1,0:T(8,128)(2,1)S(1)}, bf16[1,512,2048]{2,1,0:T(8,128)(2,1)}, u32[]{:S(2)}) copy-start(bf16[1,512,2048]{2,1,0:T(8,128)(2,1)} %param.14) | copy-start | bytes 6291460
  7.2 7.3 %copy-start.11 = (bf16[1,512,512]{2,1,0:T(8,128)(2,1)S(1)}, bf16[1,512,512]{2,1,0:T(8,128)(2,1)}, u32[]{:S(2)}) copy-start(bf16[1,512,512]{2,1,0:T(8,128)(2,1)} %param.15) | copy-start | bytes 1572868
  7.2 105.2 %all-gather.6.cloned.1.call-start = ((), (), s32[]{:S(2)}) async-start(), calls=%async_computation.2 | async-start | bytes 2621440 | tf_op jit(solution)/shard_map/all_gather | solution.py:12
  10.3 10.4 %copy-start.14 = (f32[512,8]{0,1:T(8,128)}, f32[512,8]{0,1:T(8,128)S(1)}, u32[]{:S(2)}) copy-start(f32[512,8]{0,1:T(8,128)S(1)} %get-tuple-element.525) | copy-start | bytes 49156
  11.3 13.8 %copy-start.21 = (f32[512,8]{0,1:T(8,128)}, f32[512,8]{0,1:T(8,128)S(1)}, u32[]{:S(2)}) copy-start(f32[512,8]{0,1:T(8,128)S(1)} %get-tuple-element.541) | copy-start | bytes 49156
  11.3 15.4 %copy-start.19 = (f32[512,8]{0,1:T(8,128)}, f32[512,8]{0,1:T(8,128)S(1)}, u32[]{:S(2)}) copy-start(f32[512,8]{0,1:T(8,128)S(1)} %get-tuple-element.523) | copy-start | bytes 49156
  11.9 4.4 %copy-start.16 = (f32[512,8]{0,1:T(8,128)}, f32[512,8]{0,1:T(8,128)S(1)}, u32[]{:S(2)}) copy-start(f32[512,8]{0,1:T(8,128)S(1)} %exponential_bitcast_fusion) | copy-start | bytes 49156
  19.8 7.0 %copy-start.5 = (bf16[1,512,512]{1,2,0:T(8,128)(2,1)}, bf16[1,512,512]{1,2,0:T(8,128)(2,1)S(1)}, u32[]{:S(2)}) copy-start(bf16[1,512,512]{1,2,0:T(8,128)(2,1)S(1)} %copy.48) | copy-start | bytes 1572868
  23.3 104.5 %all-gather.4.cloned.1.call-start = ((), (), s32[]{:S(2)}) async-start(), calls=%async_computation.1 | async-start | bytes 2621440 | tf_op jit(solution)/shard_map/all_gather | solution.py:12
  27.4 3.3 %copy-start.13 = (bf16[512,64]{0,1:T(8,128)(2,1)S(1)}, bf16[512,64]{0,1:T(8,128)(2,1)}, u32[]{:S(2)}) copy-start(bf16[512,64]{0,1:T(8,128)(2,1)} %get-tuple-element.539) | copy-start | bytes 196612
  28.3 157.0 %all-reduce.3.cloned.1.call-start = ((), (), s32[]{:S(2)}) async-start(), calls=%async_computation.3 | async-start | bytes 262144 | tf_op jit(solution)/shard_map/psum | solution.py:144
  30.8 57.5 %copy-start.17 = (f32[512,8]{0,1:T(8,128)S(1)}, f32[512,8]{0,1:T(8,128)}, u32[]{:S(2)}) copy-start(f32[512,8]{0,1:T(8,128)} %copy-done.16) | copy-start | bytes 49156
  30.8 57.5 %copy-start.22 = (f32[512,8]{0,1:T(8,128)S(1)}, f32[512,8]{0,1:T(8,128)}, u32[]{:S(2)}) copy-start(f32[512,8]{0,1:T(8,128)} %copy-done.21) | copy-start | bytes 49156
  33.2 2.8 %copy-start.10 = (f32[512,512]{1,0:T(8,128)S(1)}, f32[512,512]{1,0:T(8,128)}, u32[]{:S(2)}) copy-start(f32[512,512]{1,0:T(8,128)} %get-tuple-element.722) | copy-start | bytes 3145732 | tf_op jit(solution)/shard_map/while
  40.3 2.7 %copy-start.10 = (f32[512,512]{1,0:T(8,128)S(1)}, f32[512,512]{1,0:T(8,128)}, u32[]{:S(2)}) copy-start(f32[512,512]{1,0:T(8,128)} %get-tuple-element.722) | copy-start | bytes 3145732 | tf_op jit(solution)/shard_map/while
  43.0 2.0 copy-start.2
  47.4 2.7 %copy-start.10 = (f32[512,512]{1,0:T(8,128)S(1)}, f32[512,512]{1,0:T(8,128)}, u32[]{:S(2)}) copy-start(f32[512,512]{1,0:T(8,128)} %get-tuple-element.722) | copy-start | bytes 3145732 | tf_op jit(solution)/shard_map/while
  50.1 2.0 copy-start.2
  54.5 2.7 %copy-start.10 = (f32[512,512]{1,0:T(8,128)S(1)}, f32[512,512]{1,0:T(8,128)}, u32[]{:S(2)}) copy-start(f32[512,512]{1,0:T(8,128)} %get-tuple-element.722) | copy-start | bytes 3145732 | tf_op jit(solution)/shard_map/while
  57.2 2.0 copy-start.2
  61.6 2.7 %copy-start.10 = (f32[512,512]{1,0:T(8,128)S(1)}, f32[512,512]{1,0:T(8,128)}, u32[]{:S(2)}) copy-start(f32[512,512]{1,0:T(8,128)} %get-tuple-element.722) | copy-start | bytes 3145732 | tf_op jit(solution)/shard_map/while
  64.3 2.0 copy-start.2
  68.6 2.7 %copy-start.10 = (f32[512,512]{1,0:T(8,128)S(1)}, f32[512,512]{1,0:T(8,128)}, u32[]{:S(2)}) copy-start(f32[512,512]{1,0:T(8,128)} %get-tuple-element.722) | copy-start | bytes 3145732 | tf_op jit(solution)/shard_map/while
  71.3 2.0 copy-start.2
  75.7 2.7 %copy-start.10 = (f32[512,512]{1,0:T(8,128)S(1)}, f32[512,512]{1,0:T(8,128)}, u32[]{:S(2)}) copy-start(f32[512,512]{1,0:T(8,128)} %get-tuple-element.722) | copy-start | bytes 3145732 | tf_op jit(solution)/shard_map/while
  78.4 2.0 copy-start.2
  82.8 2.7 %copy-start.10 = (f32[512,512]{1,0:T(8,128)S(1)}, f32[512,512]{1,0:T(8,128)}, u32[]{:S(2)}) copy-start(f32[512,512]{1,0:T(8,128)} %get-tuple-element.722) | copy-start | bytes 3145732 | tf_op jit(solution)/shard_map/while
  85.5 2.0 copy-start.2
  138.4 4.3 %copy-start.7 = (f32[1,512,512]{1,2,0:T(8,128)S(1)}, f32[1,512,512]{1,2,0:T(8,128)}, u32[]{:S(2)}) copy-start(f32[1,512,512]{1,2,0:T(8,128)} %get-tuple-element.533) | copy-start | bytes 3145732
  138.4 5.2 %copy-start.8 = (f32[1,512,512]{1,2,0:T(8,128)S(1)}, f32[1,512,512]{1,2,0:T(8,128)}, u32[]{:S(2)}) copy-start(f32[1,512,512]{1,2,0:T(8,128)} %get-tuple-element.535) | copy-start | bytes 3145732
  145.1 78.4 %reduce-scatter.2.cloned.1.call-start = ((), (), s32[]{:S(2)}) async-start(), calls=%async_computation.4 | async-start | bytes 1179648 | tf_op jit(solution)/shard_map/reduce_scatter | solution.py:150
  193.5 2.0 copy-start.12
  (19 other events, 24.1 us)
Sparse Core Ops, SparseCore 0:
  23.4 48.6 all-gather.5
  73.6 44.9 all-gather.3
  145.2 40.0 all-reduce.2
  187.8 35.6 reduce-scatter.1
where the time goes:
time: 234 us; the launch traced here: 232 us
  matrix products  75.9 us (32%)
  waiting for transfers between devices  62.2 us (27%)
  other arithmetic  42.2 us (18%)
  local copies, waits for them, and re-layouts  21.3 us (9%)
  between operations  14.9 us (6%)
  blocking collectives  14.6 us (6%)
    psum x1, waiting for transfers between devices, per_device(): summed_bc = lax.psum(partial_bc.astype(jnp.bfloat16), 'head')  37.3 us
    reduce_scatter x1, waiting for transfers between devices, per_device(): lax.psum_scatter(jnp.einsum('td,tk->dk', tokens, summed_bc, preferred_ele...  24.9 us
    dot_general x8, matrix products, head_block(): y_head = jnp.dot(weights_main, x_head, preferred_element_type=jnp.float32)  19 us
    select_n x8, other arithmetic, step(): return jax.tree.map(lambda a, b: jnp.where(reached, a, b), new, before)  16.4 us
    dot_general x8, matrix products, head_block(): jnp.dot(weights_main.T, g_head, preferred_element_type=jnp.float32)  16.1 us
    unnamed x1, blocking collectives  14.6 us
    dot_general x8, matrix products, head_block(): value_scores = jnp.dot(g_head, x_head.T, preferred_element_type=jnp.float32)  10.2 us
    convert_element_type x8, other arithmetic, step(): part[at].astype(own.dtype)  9.56 us
  transfers between devices with their start and end apart: 4, of which 2 were waited for; matrix products, arithmetic and copies ran while one was open for 44% of the time, Pallas kernels for 0%

commit v1 on v0

--- a/solution.py
+++ b/solution.py
@@ -141,7 +141,7 @@
     y_out = (local_y + carry_y + skip_gain[None, :, None] * x_float).astype(jnp.bfloat16)
     grad_values = (local_gv + carry_gv + skip_gain[None, :, None] * g_float).astype(jnp.bfloat16)
     partial_bc = jnp.concatenate([local_gb + carry_gb, local_gc + carry_gc], axis=1)
-    summed_bc = lax.psum(partial_bc.astype(jnp.bfloat16), "head")
+    summed_bc = jnp.sum(lax.all_gather(partial_bc.astype(jnp.bfloat16), "head"), axis=0)
     grad_input = jnp.einsum(
         "tk,dk->td", summed_bc, w_bc, preferred_element_type=jnp.float32
     ).astype(jnp.bfloat16)

time: 234 us -> 201 us (0.86)
  waiting for transfers between devices: 62.2 us -> 22 us
  blocking collectives: 14.6 us -> 24.7 us
  other arithmetic: 42.2 us -> 37.2 us
  matrix products: 75.9 us -> 79.3 us
    psum x1 -> x0, waiting for transfers between devices: 37.3 us -> none  [per_device(): summed_bc = lax.psum(partial_bc.astype(jnp.bfloat16), 'head')]
    all_gather x0 -> x1, blocking collectives: none -> 10.7 us  [per_device(): lax.all_gather(partial_bc.astype(jnp.bfloat16), 'head')]
    dynamic_slice x8, local copies, waits for them, and re-layouts: 5.85 us -> 0.07 us  [per_device(): lax.scan(head_block, (zero_rows, zero_rows), head_inputs)]
    while x48, local copies, waits for them, and re-layouts: 0.78 us -> 6.46 us
    dot_general x4, matrix products: 5.96 us -> 9.34 us  [head_query(): return jnp.einsum('thp,hnp->tn', query_rows, state, precision=maximum_level)]
    reduce_scatter x1, waiting for transfers between devices: 24.9 us -> 22 us  [per_device(): lax.psum_scatter(jnp.einsum('td,tk->dk', tokens, summed_bc, preferred_ele...]
    unnamed x56 -> x42, local copies, waits for them, and re-layouts: 9.06 us -> 8 us
  transfers between devices with their start and end apart: 4 -> 3, of which waited for: 2 -> 1; matrix products, arithmetic and copies ran while one was open for 44% -> 46% of each run, Pallas kernels for 0% -> 0%
where the time goes in v1:
time: 201 us; the launch traced here: 199 us
  matrix products  79.3 us (39%)
  other arithmetic  37.2 us (19%)
  blocking collectives  24.7 us (12%)
  waiting for transfers between devices  22 us (11%)
  local copies, waits for them, and re-layouts  20.7 us (10%)
  between operations  14.8 us (7%)
    reduce_scatter x1, waiting for transfers between devices, per_device(): lax.psum_scatter(jnp.einsum('td,tk->dk', tokens, summed_bc, preferred_ele...  22 us
    dot_general x8, matrix products, head_block(): y_head = jnp.dot(weights_main, x_head, preferred_element_type=jnp.float32)  19 us
    dot_general x8, matrix products, head_block(): jnp.dot(weights_main.T, g_head, preferred_element_type=jnp.float32)  16.1 us
    select_n x8, other arithmetic, step(): return jax.tree.map(lambda a, b: jnp.where(reached, a, b), new, before)  15.9 us
    unnamed x1, blocking collectives  14 us
    all_gather x1, blocking collectives, per_device(): lax.all_gather(partial_bc.astype(jnp.bfloat16), 'head')  10.7 us
    dot_general x8, matrix products, head_block(): value_scores = jnp.dot(g_head, x_head.T, preferred_element_type=jnp.float32)  10.1 us
    dot_general x4, matrix products, head_query(): return jnp.einsum('thp,hnp->tn', query_rows, state, precision=maximum_level)  9.34 us
  transfers between devices with their start and end apart: 3, of which 1 were waited for; matrix products, arithmetic and copies ran while one was open for 46% of the time, Pallas kernels for 0%

profile of v1, /device:TPU:0, one launch (start us, length us, event | category | flops | bytes accessed | tf_op | source)
XLA Modules:
  0.0 199.4 jit_solution(17023582077168822982)
XLA Ops:
  16.1 2.0 %copy.48 = bf16[1,512,512]{1,2,0:T(8,128)(2,1)} copy(bf16[1,512,512]{2,1,0:T(8,128)(2,1)} %param.21) | data formatting | bytes 1048576 | tf_op args[7]
  32.3 2.7 %convert_multiply_fusion.7 = (f32[1,512,512]{1,2,0:T(8,128)}, f32[1,512,512]{1,2,0:T(8,128)}) fusion(bf16[1,512,512]{1,2,0:T(8,128)(2,1)} %copy.48, f32[512,8]{0,1:T(8,128)S(1)} %get-tuple-element.525, f32[512,8]{0,1:T(8,128)S(1)} %get-tuple-element.523), kind=kLoop, calls=%fused_computation.46 | loop fusion | flops 786432 | bytes 2654208 | tf_op jit(solution)/shard_map/mul | solution.py:110
  36.5 14.0 %all-reduce = bf16[32]{0:T(256)(128)(2,1)S(1)} all-reduce(bf16[32]{0:T(256)(128)(2,1)S(1)} %dynamic-update-slice), channel_id=2, replica_groups=mesh['dp'=2,'head'=4,'seq'=4] {'seq'}, use_global_device_ids=true, to_apply=%add | all-reduce | flops 32 | bytes 128
  51.3 56.6 %while.50 = (s32[]{:T(128)}, f32[512,64]{0,1:T(8,128)S(1)}, f32[512,64]{0,1:T(8,128)S(1)}, f32[8,512,64]{1,2,0:T(8,128)}, f32[8,512,64]{1,2,0:T(8,128)}, /*index...) while((s32[]{:T(128)}, f32[512,64]{0,1:T(8,128)S(1)}, ...), condition=%wide.region_3.4_spmd.clone.clone, body=%wide.region_2.3_spmd.clone.clone.sunk | while | flops 174981120 | bytes 13274344 | solution.py:90
  54.0 2.4 %fusion.141 = f32[8,512,64]{1,2,0:T(8,128)} fusion(f32[8,512,64]{1,2,0:T(8,128)} %get-tuple-element.700, s32[]{:T(128)} %get-tuple-element.697, bf16[8,512,64]{1,2,0:T(8,128)(2,1)} %copy-done.2, f32[512,512]{1,0:T(8,128)} %get-tuple-element.722, f32[512]{0:T(512)S(1)} %bitcast.273, f32[512]{0:T(512)S(1)} %bitcast.276), kind=kOutput, calls=%fused_computation.15.clone.1 | convolution fusion | flops 35913728 | bytes 1254400 | tf_op jit(solution)/shard_map/while/body/eval_jaxpr/dot_general | solution.py:82
  56.4 2.0 %fusion.142 = f32[8,512,64]{1,2,0:T(8,128)} fusion(f32[8,512,64]{1,2,0:T(8,128)} %get-tuple-element.701, s32[]{:T(128)} %get-tuple-element.697, bf16[8,512,64]{1,2,0:T(8,128)(2,1)} %get-tuple-element.716, f32[512,512]{1,0:T(8,128)S(1)} %copy-done.10, f32[512]{0:T(512)S(1)} %bitcast.274, f32[512]{0:T(512)S(1)} %bitcast.277), kind=kOutput, calls=%fused_computation.13.clone.1 | convolution fusion | flops 35913728 | bytes 1254400 | tf_op jit(solution)/shard_map/while/body/eval_jaxpr/dot_general | solution.py:83
  61.1 2.4 %fusion.141 = f32[8,512,64]{1,2,0:T(8,128)} fusion(f32[8,512,64]{1,2,0:T(8,128)} %get-tuple-element.700, s32[]{:T(128)} %get-tuple-element.697, bf16[8,512,64]{1,2,0:T(8,128)(2,1)} %copy-done.2, f32[512,512]{1,0:T(8,128)} %get-tuple-element.722, f32[512]{0:T(512)S(1)} %bitcast.273, f32[512]{0:T(512)S(1)} %bitcast.276), kind=kOutput, calls=%fused_computation.15.clone.1 | convolution fusion | flops 35913728 | bytes 1254400 | tf_op jit(solution)/shard_map/while/body/eval_jaxpr/dot_general | solution.py:82
  63.5 2.0 %fusion.142 = f32[8,512,64]{1,2,0:T(8,128)} fusion(f32[8,512,64]{1,2,0:T(8,128)} %get-tuple-element.701, s32[]{:T(128)} %get-tuple-element.697, bf16[8,512,64]{1,2,0:T(8,128)(2,1)} %get-tuple-element.716, f32[512,512]{1,0:T(8,128)S(1)} %copy-done.10, f32[512]{0:T(512)S(1)} %bitcast.274, f32[512]{0:T(512)S(1)} %bitcast.277), kind=kOutput, calls=%fused_computation.13.clone.1 | convolution fusion | flops 35913728 | bytes 1254400 | tf_op jit(solution)/shard_map/while/body/eval_jaxpr/dot_general | solution.py:83
  68.2 2.4 %fusion.141 = f32[8,512,64]{1,2,0:T(8,128)} fusion(f32[8,512,64]{1,2,0:T(8,128)} %get-tuple-element.700, s32[]{:T(128)} %get-tuple-element.697, bf16[8,512,64]{1,2,0:T(8,128)(2,1)} %copy-done.2, f32[512,512]{1,0:T(8,128)} %get-tuple-element.722, f32[512]{0:T(512)S(1)} %bitcast.273, f32[512]{0:T(512)S(1)} %bitcast.276), kind=kOutput, calls=%fused_computation.15.clone.1 | convolution fusion | flops 35913728 | bytes 1254400 | tf_op jit(solution)/shard_map/while/body/eval_jaxpr/dot_general | solution.py:82
  70.5 2.0 %fusion.142 = f32[8,512,64]{1,2,0:T(8,128)} fusion(f32[8,512,64]{1,2,0:T(8,128)} %get-tuple-element.701, s32[]{:T(128)} %get-tuple-element.697, bf16[8,512,64]{1,2,0:T(8,128)(2,1)} %get-tuple-element.716, f32[512,512]{1,0:T(8,128)S(1)} %copy-done.10, f32[512]{0:T(512)S(1)} %bitcast.274, f32[512]{0:T(512)S(1)} %bitcast.277), kind=kOutput, calls=%fused_computation.13.clone.1 | convolution fusion | flops 35913728 | bytes 1254400 | tf_op jit(solution)/shard_map/while/body/eval_jaxpr/dot_general | solution.py:83
  75.2 2.4 %fusion.141 = f32[8,512,64]{1,2,0:T(8,128)} fusion(f32[8,512,64]{1,2,0:T(8,128)} %get-tuple-element.700, s32[]{:T(128)} %get-tuple-element.697, bf16[8,512,64]{1,2,0:T(8,128)(2,1)} %copy-done.2, f32[512,512]{1,0:T(8,128)} %get-tuple-element.722, f32[512]{0:T(512)S(1)} %bitcast.273, f32[512]{0:T(512)S(1)} %bitcast.276), kind=kOutput, calls=%fused_computation.15.clone.1 | convolution fusion | flops 35913728 | bytes 1254400 | tf_op jit(solution)/shard_map/while/body/eval_jaxpr/dot_general | solution.py:82
  77.6 2.0 %fusion.142 = f32[8,512,64]{1,2,0:T(8,128)} fusion(f32[8,512,64]{1,2,0:T(8,128)} %get-tuple-element.701, s32[]{:T(128)} %get-tuple-element.697, bf16[8,512,64]{1,2,0:T(8,128)(2,1)} %get-tuple-element.716, f32[512,512]{1,0:T(8,128)S(1)} %copy-done.10, f32[512]{0:T(512)S(1)} %bitcast.274, f32[512]{0:T(512)S(1)} %bitcast.277), kind=kOutput, calls=%fused_computation.13.clone.1 | convolution fusion | flops 35913728 | bytes 1254400 | tf_op jit(solution)/shard_map/while/body/eval_jaxpr/dot_general | solution.py:83
  82.3 2.4 %fusion.141 = f32[8,512,64]{1,2,0:T(8,128)} fusion(f32[8,512,64]{1,2,0:T(8,128)} %get-tuple-element.700, s32[]{:T(128)} %get-tuple-element.697, bf16[8,512,64]{1,2,0:T(8,128)(2,1)} %copy-done.2, f32[512,512]{1,0:T(8,128)} %get-tuple-element.722, f32[512]{0:T(512)S(1)} %bitcast.273, f32[512]{0:T(512)S(1)} %bitcast.276), kind=kOutput, calls=%fused_computation.15.clone.1 | convolution fusion | flops 35913728 | bytes 1254400 | tf_op jit(solution)/shard_map/while/body/eval_jaxpr/dot_general | solution.py:82
  89.4 2.4 %fusion.141 = f32[8,512,64]{1,2,0:T(8,128)} fusion(f32[8,512,64]{1,2,0:T(8,128)} %get-tuple-element.700, s32[]{:T(128)} %get-tuple-element.697, bf16[8,512,64]{1,2,0:T(8,128)(2,1)} %copy-done.2, f32[512,512]{1,0:T(8,128)} %get-tuple-element.722, f32[512]{0:T(512)S(1)} %bitcast.273, f32[512]{0:T(512)S(1)} %bitcast.276), kind=kOutput, calls=%fused_computation.15.clone.1 | convolution fusion | flops 35913728 | bytes 1254400 | tf_op jit(solution)/shard_map/while/body/eval_jaxpr/dot_general | solution.py:82
  91.7 2.0 %fusion.142 = f32[8,512,64]{1,2,0:T(8,128)} fusion(f32[8,512,64]{1,2,0:T(8,128)} %get-tuple-element.701, s32[]{:T(128)} %get-tuple-element.697, bf16[8,512,64]{1,2,0:T(8,128)(2,1)} %get-tuple-element.716, f32[512,512]{1,0:T(8,128)S(1)} %copy-done.10, f32[512]{0:T(512)S(1)} %bitcast.274, f32[512]{0:T(512)S(1)} %bitcast.277), kind=kOutput, calls=%fused_computation.13.clone.1 | convolution fusion | flops 35913728 | bytes 1254400 | tf_op jit(solution)/shard_map/while/body/eval_jaxpr/dot_general | solution.py:83
  96.4 2.4 %fusion.141 = f32[8,512,64]{1,2,0:T(8,128)} fusion(f32[8,512,64]{1,2,0:T(8,128)} %get-tuple-element.700, s32[]{:T(128)} %get-tuple-element.697, bf16[8,512,64]{1,2,0:T(8,128)(2,1)} %copy-done.2, f32[512,512]{1,0:T(8,128)} %get-tuple-element.722, f32[512]{0:T(512)S(1)} %bitcast.273, f32[512]{0:T(512)S(1)} %bitcast.276), kind=kOutput, calls=%fused_computation.15.clone.1 | convolution fusion | flops 35913728 | bytes 1254400 | tf_op jit(solution)/shard_map/while/body/eval_jaxpr/dot_general | solution.py:82
  98.8 2.0 %fusion.142 = f32[8,512,64]{1,2,0:T(8,128)} fusion(f32[8,512,64]{1,2,0:T(8,128)} %get-tuple-element.701, s32[]{:T(128)} %get-tuple-element.697, bf16[8,512,64]{1,2,0:T(8,128)(2,1)} %get-tuple-element.716, f32[512,512]{1,0:T(8,128)S(1)} %copy-done.10, f32[512]{0:T(512)S(1)} %bitcast.274, f32[512]{0:T(512)S(1)} %bitcast.277), kind=kOutput, calls=%fused_computation.13.clone.1 | convolution fusion | flops 35913728 | bytes 1254400 | tf_op jit(solution)/shard_map/while/body/eval_jaxpr/dot_general | solution.py:83
  103.5 2.4 %fusion.141 = f32[8,512,64]{1,2,0:T(8,128)} fusion(f32[8,512,64]{1,2,0:T(8,128)} %get-tuple-element.700, s32[]{:T(128)} %get-tuple-element.697, bf16[8,512,64]{1,2,0:T(8,128)(2,1)} %copy-done.2, f32[512,512]{1,0:T(8,128)} %get-tuple-element.722, f32[512]{0:T(512)S(1)} %bitcast.273, f32[512]{0:T(512)S(1)} %bitcast.276), kind=kOutput, calls=%fused_computation.15.clone.1 | convolution fusion | flops 35913728 | bytes 1254400 | tf_op jit(solution)/shard_map/while/body/eval_jaxpr/dot_general | solution.py:82
  108.7 12.8 %while.49 = (s32[]{:T(128)}, f32[4,8,64,64]{3,2,1,0:T(8,128)}, s32[]{:T(128)}, bf16[4,8]{1,0:T(4,128)(2,1)}, bf16[4,4,8,64,64]{4,3,2,1,0:T(8,128)(2,1)}, /*index=5*/s32[]{:T(128)}, s32[]{:T(128)}, s32[]{:T(128)}, s32[]{:T(128)}) while((s32[]{:T(128)}, f32[4,8,64,64]{3,2,1,0:T(8,128)}, s32[]{:T(128)}, bf16[4,8]{1,0:T(4,128)(2,1)}, ...), condition=%wide.region_7.8_spmd.clone, body=%wide.region_6.7_spmd.clone.sunk | while | flops 655376 | bytes 1310967 | solution.py:26
  109.4 2.3 %fusion.131 = f32[4,8,64,64]{3,2,1,0:T(8,128)} fusion(f32[4,8,64,64]{3,2,1,0:T(8,128)} %get-tuple-element.735, bf16[4,4,8,64,64]{4,3,2,1,0:T(8,128)(2,1)} %get-tuple-element.747, s32[]{:T(128)S(6)} %select_n.121, f32[8]{0:T(128)S(1)} %bitcast_convert_fusion.5, pred[]{:T(512)S(6)} %compare.10, pred[]{:T(512)S(6)} %gt.12), kind=kLoop, calls=%fused_computation.6.clone.1 | loop fusion | flops 655360 | bytes 1310758 | tf_op jit(solution)/shard_map/while/body/eval_jaxpr/jit(_where)/select_n | solution.py:24
  112.4 2.6 %fusion.131 = f32[4,8,64,64]{3,2,1,0:T(8,128)} fusion(f32[4,8,64,64]{3,2,1,0:T(8,128)} %get-tuple-element.735, bf16[4,4,8,64,64]{4,3,2,1,0:T(8,128)(2,1)} %get-tuple-element.747, s32[]{:T(128)S(6)} %select_n.121, f32[8]{0:T(128)S(1)} %bitcast_convert_fusion.5, pred[]{:T(512)S(6)} %compare.10, pred[]{:T(512)S(6)} %gt.12), kind=kLoop, calls=%fused_computation.6.clone.1 | loop fusion | flops 655360 | bytes 1310758 | tf_op jit(solution)/shard_map/while/body/eval_jaxpr/jit(_where)/select_n | solution.py:24
  115.7 2.6 %fusion.131 = f32[4,8,64,64]{3,2,1,0:T(8,128)} fusion(f32[4,8,64,64]{3,2,1,0:T(8,128)} %get-tuple-element.735, bf16[4,4,8,64,64]{4,3,2,1,0:T(8,128)(2,1)} %get-tuple-element.747, s32[]{:T(128)S(6)} %select_n.121, f32[8]{0:T(128)S(1)} %bitcast_convert_fusion.5, pred[]{:T(512)S(6)} %compare.10, pred[]{:T(512)S(6)} %gt.12), kind=kLoop, calls=%fused_computation.6.clone.1 | loop fusion | flops 655360 | bytes 1310758 | tf_op jit(solution)/shard_map/while/body/eval_jaxpr/jit(_where)/select_n | solution.py:24
  118.9 2.6 %fusion.131 = f32[4,8,64,64]{3,2,1,0:T(8,128)} fusion(f32[4,8,64,64]{3,2,1,0:T(8,128)} %get-tuple-element.735, bf16[4,4,8,64,64]{4,3,2,1,0:T(8,128)(2,1)} %get-tuple-element.747, s32[]{:T(128)S(6)} %select_n.121, f32[8]{0:T(128)S(1)} %bitcast_convert_fusion.5, pred[]{:T(512)S(6)} %compare.10, pred[]{:T(512)S(6)} %gt.12), kind=kLoop, calls=%fused_computation.6.clone.1 | loop fusion | flops 655360 | bytes 1310758 | tf_op jit(solution)/shard_map/while/body/eval_jaxpr/jit(_where)/select_n | solution.py:24
  121.5 2.6 %copy.55 = f32[4,8,64,64]{2,3,1,0:T(8,128)} copy(f32[4,8,64,64]{3,2,1,0:T(8,128)} %get-tuple-element.313) | data formatting | bytes 1048576 | tf_op jit(solution)/shard_map/while | solution.py:26
  124.2 2.7 %convolution_bitcast_fusion.5 = f32[512,64]{0,1:T(8,128)} fusion(f32[512,8,64]{0,2,1:T(8,128)} %bitcast.265, f32[4,8,64,64]{3,2,1,0:T(8,128)} %get-tuple-element.313), kind=kOutput, calls=%fused_computation.64 | convolution fusion | flops 201326592 | bytes 1441792 | tf_op jit(solution)/shard_map/thp,hnp->tn/dot_general | solution.py:51
  126.9 10.9 %while.48 = (s32[]{:T(128)}, f32[4,8,64,64]{3,2,1,0:T(8,128)S(1)}, s32[]{:T(128)}, bf16[4,8]{1,0:T(4,128)(2,1)}, bf16[4,4,8,64,64]{4,3,2,1,0:T(8,128)(2,1)}, /*index=5*/s32[]{:T(128)}, s32[]{:T(128)}) while((s32[]{:T(128)}, f32[4,8,64,64]{3,2,1,0:T(8,128)S(1)}, s32[]{:T(128)}, bf16[4,8]{1,0:T(4,128)(2,1)}, ...), condition=%wide.region_5.6_spmd.clone, body=%wide.region_4.5_spmd.clone.sunk | while | flops 655372 | bytes 1310905 | solution.py:26
  137.9 2.7 %convolution_bitcast_fusion.3 = f32[512,64]{0,1:T(8,128)} fusion(f32[512,8,64]{0,2,1:T(8,128)} %bitcast.264, f32[4,8,64,64]{3,2,1,0:T(8,128)} %get-tuple-element.313), kind=kOutput, calls=%fused_computation.62 | convolution fusion | flops 201326592 | bytes 1441792 | tf_op jit(solution)/shard_map/thp,hnp->tn/dot_general | solution.py:51
  141.9 2.1 %fusion.41 = bf16[1,512,64]{1,2,0:T(8,128)(2,1)S(1)} fusion(f32[512,64]{0,1:T(8,128)S(1)} %get-tuple-element.315, f32[512,64]{0,1:T(8,128)} %convolution_bitcast_fusion.5, f32[512,8,64]{0,2,1:T(8,128)} %bitcast.262, f32[4,8,64,64]{3,2,1,0:T(8,128)S(1)} %get-tuple-element.312), kind=kOutput, calls=%fused_computation.76 | convolution fusion | flops 201424896 | bytes 1638400 | tf_op jit(solution)/shard_map/thp,hnp->tn/dot_general | solution.py:51
  145.9 10.7 %all_gather.21 = bf16[4,512,128]{2,1,0:T(8,128)(2,1)S(1)} all-gather(bf16[1,512,128]{2,1,0:T(8,128)(2,1)S(1)} %copy.60), channel_id=1, replica_groups=mesh['dp'=2,'head'=4,'seq'=4] {'head'}, dimensions={0}, use_global_device_ids=true | all-gather | bytes 655360 | tf_op jit(solution)/shard_map/all_gather | solution.py:144
  161.8 2.3 %fusion.46 = (bf16[512,8,64]{0,2,1:T(8,128)(2,1)S(1)}, bf16[512,8,64]{0,2,1:T(8,128)(2,1)S(1)}) fusion(bf16[512,8,64]{0,2,1:T(8,128)(2,1)S(1)} %bitcast.257, f32[8,512,64]{1,2,0:T(8,128)} %get-tuple-element.314, f32[512,8,64]{0,2,1:T(8,128)S(1)} %bitcast.261, f32[512,8,64]{0,2,1:T(8,128)S(1)} %bitcast.259, f32[8]{0:T(128)S(1)} %copy-done.17, ...), kind=kLoop, calls=%fused_computation.81 | loop fusion | flops 4194304 | bytes 8454176 | tf_op jit(solution)/shard_map/convert_element_type | solution.py:142
  166.1 3.1 %fusion.20 = bf16[1,512,2048]{2,1,0:T(8,128)(2,1)} fusion(bf16[512,128]{1,0:T(8,128)(2,1)S(1)} %reduce_sum.12, bf16[2048,128]{1,0:T(8,128)(2,1)} %param.17), kind=kOutput, calls=%fused_computation.34 | convolution fusion | flops 269484032 | bytes 2752512 | tf_op jit(solution)/shard_map/tk,dk->td/dot_general | solution.py:145
  169.2 22.0 %reduce-scatter.2.cloned.1.call-done = f32[256,128]{0,1:T(8,128)} async-done(((f32[2048,128]{0,1:T(8,128)}), f32[256,128]{0,1:T(8,128)}) %reduce-scatter.2.cloned.1.call-update) | async-done | bytes 131088 | tf_op jit(solution)/shard_map/reduce_scatter | solution.py:150
  (188 shorter events, 75.9 us)
Async XLA Ops:
  7.2 4.2 %copy-start = (bf16[1,512,2048]{2,1,0:T(8,128)(2,1)S(1)}, bf16[1,512,2048]{2,1,0:T(8,128)(2,1)}, u32[]{:S(2)}) copy-start(bf16[1,512,2048]{2,1,0:T(8,128)(2,1)} %param.14) | copy-start | bytes 6291460
  7.2 100.8 %all-gather.6.cloned.1.call-start = ((), (), s32[]{:S(2)}) async-start(), calls=%async_computation.2 | async-start | bytes 2621440 | tf_op jit(solution)/shard_map/all_gather | solution.py:12
  11.3 17.9 %copy-start.15 = (f32[512,8]{0,1:T(8,128)}, f32[512,8]{0,1:T(8,128)S(1)}, u32[]{:S(2)}) copy-start(f32[512,8]{0,1:T(8,128)S(1)} %get-tuple-element.541) | copy-start | bytes 49156
  11.3 21.0 %copy-start.13 = (f32[512,8]{0,1:T(8,128)}, f32[512,8]{0,1:T(8,128)S(1)}, u32[]{:S(2)}) copy-start(f32[512,8]{0,1:T(8,128)S(1)} %get-tuple-element.523) | copy-start | bytes 49156
  11.3 17.9 %copy-start.11 = (f32[512,8]{0,1:T(8,128)}, f32[512,8]{0,1:T(8,128)S(1)}, u32[]{:S(2)}) copy-start(f32[512,8]{0,1:T(8,128)S(1)} %exponential_bitcast_fusion) | copy-start | bytes 49156
  22.7 104.2 %all-gather.4.cloned.1.call-start = ((), (), s32[]{:S(2)}) async-start(), calls=%async_computation.1 | async-start | bytes 2621440 | tf_op jit(solution)/shard_map/all_gather | solution.py:12
  29.0 162.2 %reduce-scatter.2.cloned.1.call-start = ((), (), s32[]{:S(2)}) async-start(), calls=%async_computation.3 | async-start | bytes 1179648 | tf_op jit(solution)/shard_map/reduce_scatter | solution.py:150
  31.0 4.0 %copy-start.18 = (u32[32]{0:T(128)S(1)}, u32[32]{0:T(128)}, u32[]{:S(2)}) copy-start(u32[32]{0:T(128)} %constant.108) | copy-start | bytes 388
  53.7 2.7 %copy-start.10 = (f32[512,512]{1,0:T(8,128)S(1)}, f32[512,512]{1,0:T(8,128)}, u32[]{:S(2)}) copy-start(f32[512,512]{1,0:T(8,128)} %get-tuple-element.722) | copy-start | bytes 3145732 | tf_op jit(solution)/shard_map/while
  56.4 2.0 %copy-start.3 = (bf16[8,512,64]{1,2,0:T(8,128)(2,1)S(1)}, bf16[8,512,64]{1,2,0:T(8,128)(2,1)}, u32[]{:S(2)}) copy-start(bf16[8,512,64]{1,2,0:T(8,128)(2,1)} %copy-done.2) | copy-start | bytes 1572868 | tf_op jit(solution)/shard_map/while
  60.8 2.7 %copy-start.10 = (f32[512,512]{1,0:T(8,128)S(1)}, f32[512,512]{1,0:T(8,128)}, u32[]{:S(2)}) copy-start(f32[512,512]{1,0:T(8,128)} %get-tuple-element.722) | copy-start | bytes 3145732 | tf_op jit(solution)/shard_map/while
  63.5 2.0 %copy-start.3 = (bf16[8,512,64]{1,2,0:T(8,128)(2,1)S(1)}, bf16[8,512,64]{1,2,0:T(8,128)(2,1)}, u32[]{:S(2)}) copy-start(bf16[8,512,64]{1,2,0:T(8,128)(2,1)} %copy-done.2) | copy-start | bytes 1572868 | tf_op jit(solution)/shard_map/while
  67.8 2.7 %copy-start.10 = (f32[512,512]{1,0:T(8,128)S(1)}, f32[512,512]{1,0:T(8,128)}, u32[]{:S(2)}) copy-start(f32[512,512]{1,0:T(8,128)} %get-tuple-element.722) | copy-start | bytes 3145732 | tf_op jit(solution)/shard_map/while
  70.5 2.0 %copy-start.3 = (bf16[8,512,64]{1,2,0:T(8,128)(2,1)S(1)}, bf16[8,512,64]{1,2,0:T(8,128)(2,1)}, u32[]{:S(2)}) copy-start(bf16[8,512,64]{1,2,0:T(8,128)(2,1)} %copy-done.2) | copy-start | bytes 1572868 | tf_op jit(solution)/shard_map/while
  74.9 2.7 %copy-start.10 = (f32[512,512]{1,0:T(8,128)S(1)}, f32[512,512]{1,0:T(8,128)}, u32[]{:S(2)}) copy-start(f32[512,512]{1,0:T(8,128)} %get-tuple-element.722) | copy-start | bytes 3145732 | tf_op jit(solution)/shard_map/while
  77.6 2.0 %copy-start.3 = (bf16[8,512,64]{1,2,0:T(8,128)(2,1)S(1)}, bf16[8,512,64]{1,2,0:T(8,128)(2,1)}, u32[]{:S(2)}) copy-start(bf16[8,512,64]{1,2,0:T(8,128)(2,1)} %copy-done.2) | copy-start | bytes 1572868 | tf_op jit(solution)/shard_map/while
  82.0 2.7 %copy-start.10 = (f32[512,512]{1,0:T(8,128)S(1)}, f32[512,512]{1,0:T(8,128)}, u32[]{:S(2)}) copy-start(f32[512,512]{1,0:T(8,128)} %get-tuple-element.722) | copy-start | bytes 3145732 | tf_op jit(solution)/shard_map/while
  84.7 2.0 %copy-start.3 = (bf16[8,512,64]{1,2,0:T(8,128)(2,1)S(1)}, bf16[8,512,64]{1,2,0:T(8,128)(2,1)}, u32[]{:S(2)}) copy-start(bf16[8,512,64]{1,2,0:T(8,128)(2,1)} %copy-done.2) | copy-start | bytes 1572868 | tf_op jit(solution)/shard_map/while
  89.0 2.7 %copy-start.10 = (f32[512,512]{1,0:T(8,128)S(1)}, f32[512,512]{1,0:T(8,128)}, u32[]{:S(2)}) copy-start(f32[512,512]{1,0:T(8,128)} %get-tuple-element.722) | copy-start | bytes 3145732 | tf_op jit(solution)/shard_map/while
  91.7 2.0 %copy-start.3 = (bf16[8,512,64]{1,2,0:T(8,128)(2,1)S(1)}, bf16[8,512,64]{1,2,0:T(8,128)(2,1)}, u32[]{:S(2)}) copy-start(bf16[8,512,64]{1,2,0:T(8,128)(2,1)} %copy-done.2) | copy-start | bytes 1572868 | tf_op jit(solution)/shard_map/while
  96.1 2.7 %copy-start.10 = (f32[512,512]{1,0:T(8,128)S(1)}, f32[512,512]{1,0:T(8,128)}, u32[]{:S(2)}) copy-start(f32[512,512]{1,0:T(8,128)} %get-tuple-element.722) | copy-start | bytes 3145732 | tf_op jit(solution)/shard_map/while
  98.8 2.0 %copy-start.3 = (bf16[8,512,64]{1,2,0:T(8,128)(2,1)S(1)}, bf16[8,512,64]{1,2,0:T(8,128)(2,1)}, u32[]{:S(2)}) copy-start(bf16[8,512,64]{1,2,0:T(8,128)(2,1)} %copy-done.2) | copy-start | bytes 1572868 | tf_op jit(solution)/shard_map/while
  103.2 2.7 %copy-start.10 = (f32[512,512]{1,0:T(8,128)S(1)}, f32[512,512]{1,0:T(8,128)}, u32[]{:S(2)}) copy-start(f32[512,512]{1,0:T(8,128)} %get-tuple-element.722) | copy-start | bytes 3145732 | tf_op jit(solution)/shard_map/while
  105.9 2.0 %copy-start.3 = (bf16[8,512,64]{1,2,0:T(8,128)(2,1)S(1)}, bf16[8,512,64]{1,2,0:T(8,128)(2,1)}, u32[]{:S(2)}) copy-start(bf16[8,512,64]{1,2,0:T(8,128)(2,1)} %copy-done.2) | copy-start | bytes 1572868 | tf_op jit(solution)/shard_map/while
  121.5 5.4 %copy-start.1 = (f32[4,8,64,64]{3,2,1,0:T(8,128)S(1)}, f32[4,8,64,64]{3,2,1,0:T(8,128)}, u32[]{:S(2)}) copy-start(f32[4,8,64,64]{3,2,1,0:T(8,128)} %custom-call) | copy-start | bytes 1572868
  141.9 2.1 %copy-start.7 = (f32[1,512,512]{1,2,0:T(8,128)S(1)}, f32[1,512,512]{1,2,0:T(8,128)}, u32[]{:S(2)}) copy-start(f32[1,512,512]{1,2,0:T(8,128)} %get-tuple-element.535) | copy-start | bytes 3145732
  156.8 2.6 %copy-start.8 = (f32[4,8,64,64]{2,3,1,0:T(8,128)S(1)}, f32[4,8,64,64]{2,3,1,0:T(8,128)}, u32[]{:S(2)}) copy-start(f32[4,8,64,64]{2,3,1,0:T(8,128)} %copy.55) | copy-start | bytes 1572868
  159.9 1.8 copy-start.5
  159.9 1.8 copy-start.6
  160.0 1.8 copy-start.9
  160.0 1.8 copy-start.12
  160.0 1.8 copy-start.14
  (11 other events, 10.9 us)
Sparse Core Ops, SparseCore 0:
  22.8 48.8 all-gather.5
  73.3 44.6 all-gather.3
  158.4 32.7 reduce-scatter.1
